TPU v7x, 32 devices: a whole 2x2x4 slice. The times are simulated.
32 devices in a mesh: parts: 1, query: 16 (over z, y, x), blk: 2 (over core).
Axes of the slice: x: 2, y: 2, z: 4, core: 2. Of those that a mesh axis runs over, the one named last changes fastest.
Arguments:
- queries: bfloat16 [2, 256, 16384], P('blk', ('parts', 'query')), may hold values from -600 to 600, as said below
- cameras: bfloat16 [16, 512, 16384], P(('parts', 'query'), 'blk'), may hold values from -600 to 600, as said below
- query_block: int32 [16, 2, 16], P(('parts', 'query'), 'blk'), may hold values from 0 to 1
- camera_block: int32 [16, 2, 16], P(('parts', 'query'), 'blk'), may hold values from 0 to 3
- counts: int32 [16, 2], P(('parts', 'query'), 'blk'), may hold values from 1 to 16, as said below
Outputs:
- scores: float32 [16, 2, 16, 128, 128], P(('parts', 'query'), 'blk')
Inputs may be any that keep to these rules, and one draw needn't show every extreme that they name: `queries`: finite values. `cameras`: finite values. `counts`: in every draw some list has all 16 slots live.
All inputs are finite; a program needn't handle non-finite values.
Results may differ from a plain program's by a relative error of at most 0.0003.
Values may be sent and summed in bfloat16 or wider, within the bound.
A program may use at most 192 MiB of HBM per device.

v0:
```python
import math

import jax
import jax.numpy as jnp
from jax import lax
from jax.sharding import PartitionSpec as P

BLOCK = 128


def passed_along(x, axis, by):
    devices = lax.axis_size(axis)
    return lax.ppermute(x, axis, [(i, (i + by) % devices) for i in range(devices)])


def inverse_rms(values):
    wide = values.astype(jnp.float32)
    return lax.rsqrt(jnp.mean(wide * wide, axis=-1) + 1e-06)


def shards(queries, cameras, query_block, camera_block, counts):
    feature_count = queries.shape[2]
    block_rows = BLOCK
    panel = lax.all_gather(queries[0], "query", axis=0, tiled=True)
    query_scale = inverse_rms(panel)
    core_count = lax.axis_size("blk")
    tile_rows = cameras.shape[1]
    tile_list = [cameras[0]]
    current = cameras[0]
    current = passed_along(current, "blk", 1)
    tile_list.append(current)
    camera_stack = jnp.concatenate(tile_list, axis=0)
    camera_scale = inverse_rms(camera_stack)
    my_core = lax.axis_index("blk")
    slot_total = query_block.shape[2]
    live_slots = counts[0, 0]
    inv_root = 1.0 / math.sqrt(feature_count)

    def score_slot(slot_index, results):
        query_start = query_block[0, 0, slot_index] * block_rows
        camera_global = camera_block[0, 0, slot_index] * block_rows
        owner_core = camera_global // tile_rows
        offset_rows = camera_global % tile_rows
        cycle_turn = (my_core - owner_core) % core_count
        camera_start = cycle_turn * tile_rows + offset_rows
        query_rows = lax.dynamic_slice_in_dim(panel, query_start, block_rows, 0)
        camera_rows = lax.dynamic_slice_in_dim(camera_stack, camera_start, block_rows, 0)
        products = lax.dot_general(
            query_rows, camera_rows, (((1,), (1,)), ((), ())), preferred_element_type=jnp.float32
        )
        query_norms = lax.dynamic_slice_in_dim(query_scale, query_start, block_rows, 0)
        camera_norms = lax.dynamic_slice_in_dim(camera_scale, camera_start, block_rows, 0)
        scored = products * query_norms[:, None] * camera_norms[None, :] * inv_root
        return lax.dynamic_update_index_in_dim(results, scored, slot_index, 0)

    results = lax.fori_loop(
        0, live_slots, score_slot, jnp.zeros((slot_total, block_rows, block_rows), jnp.float32)
    )
    return results[None, None]


def solution(mesh):
    placed = (
        P("blk", ("parts", "query"), None),
        P(("parts", "query"), "blk", None),
        P(("parts", "query"), "blk", None),
        P(("parts", "query"), "blk", None),
        P(("parts", "query"), "blk"),
    )
    return jax.shard_map(
        shards,
        mesh=mesh,
        in_specs=placed,
        out_specs=P(("parts", "query"), "blk", None, None, None),
        check_vma=False,
    )
```

profile of v0, /device:TPU:4, one launch (start us, length us, event | category | flops | bytes accessed | tf_op | source)
XLA Modules:
  0.0 304.3 jit_solution(10513318406988686946)
XLA Ops:
  6.5 0.7 all-gather.3.cloned.1.call-update
  7.3 13.5 %collective-permute-done = bf16[256,16384]{1,0:T(8,128)(2,1)} collective-permute-done((bf16[256,16384]{1,0:T(8,128)(2,1)}, bf16[256,16384]{1,0:T(8,128)(2,1)}, u32[]{:S(2)}, u32[]{:S(2)}) %collective-permute-start) | collective-permute-done | bytes 8388640 | tf_op jit(solution)/shard_map/ppermute | solution.py:13
  20.8 7.2 %multiply_reduce_fusion = f32[512]{0:T(512)S(1)} fusion(bf16[256,16384]{1,0:T(8,128)(2,1)} %collective-permute-done, bf16[256,16384]{1,0:T(8,128)(2,1)} %bitcast.19), kind=kLoop, calls=%fused_computation.11 | loop fusion | flops 50331136 | bytes 16779264 | tf_op jit(solution)/shard_map/reduce_sum | solution.py:18
  28.1 10.7 %pad_maximum_fusion = bf16[512,16384]{1,0:T(8,128)(2,1)} fusion(bf16[256,16384]{1,0:T(8,128)(2,1)} %collective-permute-done, bf16[256,16384]{1,0:T(8,128)(2,1)S(1)} %bitcast.20), kind=kLoop, calls=%fused_computation.12 | loop fusion | flops 33554432 | bytes 33554432 | tf_op jit(solution)/shard_map/concatenate | solution.py:32
  38.8 85.4 %all-gather.3.cloned.1.call-done = bf16[1,256,16384]{2,1,0:T(8,128)(2,1)} async-done(((bf16[1,16,16384]{2,1,0:T(8,128)(2,1)}), bf16[1,256,16384]{2,1,0:T(8,128)(2,1)}) %all-gather.3.cloned.1.call-update) | async-done | bytes 8388624 | tf_op jit(solution)/shard_map/all_gather | solution.py:24
  124.2 5.1 %multiply_reduce_fusion.1 = f32[256]{0:T(256)S(1)} fusion(bf16[1,256,16384]{2,1,0:T(8,128)(2,1)} %all-gather.3.cloned.1.call-done), kind=kLoop, calls=%fused_computation.13 | loop fusion | flops 12582656 | bytes 8389632 | tf_op jit(solution)/shard_map/reduce_sum | solution.py:18
  129.3 0.1 broadcast_in_dim.16
  129.5 167.0 %while.13 = (s32[]{:T(128)}, f32[16,128,128]{2,1,0:T(8,128)S(1)}, s32[]{:T(128)}, s32[1,1,16]{2,1,0:T(1,128)S(1)}, bf16[256,16384]{1,0:T(8,128)(2,1)}, /*index=5...) while((s32[]{:T(128)}, f32[16,128,128]{2,1,0:T(8,128)S(1)}, ...), condition=%wide.region_3.4_spmd, body=%wide.region_2.3_spmd.sunk | while | flops 536920128 | bytes 8457863 | solution.py:56
  130.1 0.6 fusion.37
  133.0 0.1 dynamic_slice.74
  135.0 0.1 dynamic_slice.75
  135.1 4.8 %fusion.38 = f32[16,128,128]{2,1,0:T(8,128)S(1)} fusion(f32[16,128,128]{2,1,0:T(8,128)S(1)} %get-tuple-element.281, s32[]{:T(128)S(6)} %select_n.63, bf16[512,16384]{1,0:T(8,128)(2,1)} %get-tuple-element.306, s32[]{:T(128)S(6)} %select_n.67, bf16[256,16384]{1,0:T(8,128)(2,1)} %get-tuple-element.303, s32[]{:T(128)S(6)} %select_n.68, ...), kind=kOutput, calls=%fused_computation.7.clone.1 | convolution fusion | flops 536920064 | bytes 8455180 | tf_op jit(solution)/shard_map/while/body/dot_general | solution.py:48
  140.5 0.6 fusion.37
  143.4 0.1 dynamic_slice.74
  145.4 0.1 dynamic_slice.75
  145.5 4.8 %fusion.38 = f32[16,128,128]{2,1,0:T(8,128)S(1)} fusion(f32[16,128,128]{2,1,0:T(8,128)S(1)} %get-tuple-element.281, s32[]{:T(128)S(6)} %select_n.63, bf16[512,16384]{1,0:T(8,128)(2,1)} %get-tuple-element.306, s32[]{:T(128)S(6)} %select_n.67, bf16[256,16384]{1,0:T(8,128)(2,1)} %get-tuple-element.303, s32[]{:T(128)S(6)} %select_n.68, ...), kind=kOutput, calls=%fused_computation.7.clone.1 | convolution fusion | flops 536920064 | bytes 8455180 | tf_op jit(solution)/shard_map/while/body/dot_general | solution.py:48
  151.0 0.6 fusion.37
  153.8 0.1 dynamic_slice.74
  155.8 0.1 dynamic_slice.75
  155.9 4.8 %fusion.38 = f32[16,128,128]{2,1,0:T(8,128)S(1)} fusion(f32[16,128,128]{2,1,0:T(8,128)S(1)} %get-tuple-element.281, s32[]{:T(128)S(6)} %select_n.63, bf16[512,16384]{1,0:T(8,128)(2,1)} %get-tuple-element.306, s32[]{:T(128)S(6)} %select_n.67, bf16[256,16384]{1,0:T(8,128)(2,1)} %get-tuple-element.303, s32[]{:T(128)S(6)} %select_n.68, ...), kind=kOutput, calls=%fused_computation.7.clone.1 | convolution fusion | flops 536920064 | bytes 8455180 | tf_op jit(solution)/shard_map/while/body/dot_general | solution.py:48
  161.4 0.6 fusion.37
  164.2 0.1 dynamic_slice.74
  166.2 0.1 dynamic_slice.75
  166.3 4.8 %fusion.38 = f32[16,128,128]{2,1,0:T(8,128)S(1)} fusion(f32[16,128,128]{2,1,0:T(8,128)S(1)} %get-tuple-element.281, s32[]{:T(128)S(6)} %select_n.63, bf16[512,16384]{1,0:T(8,128)(2,1)} %get-tuple-element.306, s32[]{:T(128)S(6)} %select_n.67, bf16[256,16384]{1,0:T(8,128)(2,1)} %get-tuple-element.303, s32[]{:T(128)S(6)} %select_n.68, ...), kind=kOutput, calls=%fused_computation.7.clone.1 | convolution fusion | flops 536920064 | bytes 8455180 | tf_op jit(solution)/shard_map/while/body/dot_general | solution.py:48
  171.8 0.6 fusion.37
  174.6 0.1 dynamic_slice.74
  176.6 0.1 dynamic_slice.75
  176.7 4.7 %fusion.38 = f32[16,128,128]{2,1,0:T(8,128)S(1)} fusion(f32[16,128,128]{2,1,0:T(8,128)S(1)} %get-tuple-element.281, s32[]{:T(128)S(6)} %select_n.63, bf16[512,16384]{1,0:T(8,128)(2,1)} %get-tuple-element.306, s32[]{:T(128)S(6)} %select_n.67, bf16[256,16384]{1,0:T(8,128)(2,1)} %get-tuple-element.303, s32[]{:T(128)S(6)} %select_n.68, ...), kind=kOutput, calls=%fused_computation.7.clone.1 | convolution fusion | flops 536920064 | bytes 8455180 | tf_op jit(solution)/shard_map/while/body/dot_general | solution.py:48
  182.1 0.6 fusion.37
  185.0 0.1 dynamic_slice.74
  186.9 0.1 dynamic_slice.75
  187.0 4.7 %fusion.38 = f32[16,128,128]{2,1,0:T(8,128)S(1)} fusion(f32[16,128,128]{2,1,0:T(8,128)S(1)} %get-tuple-element.281, s32[]{:T(128)S(6)} %select_n.63, bf16[512,16384]{1,0:T(8,128)(2,1)} %get-tuple-element.306, s32[]{:T(128)S(6)} %select_n.67, bf16[256,16384]{1,0:T(8,128)(2,1)} %get-tuple-element.303, s32[]{:T(128)S(6)} %select_n.68, ...), kind=kOutput, calls=%fused_computation.7.clone.1 | convolution fusion | flops 536920064 | bytes 8455180 | tf_op jit(solution)/shard_map/while/body/dot_general | solution.py:48
  192.4 0.6 fusion.37
  195.3 0.1 dynamic_slice.74
  197.3 0.1 dynamic_slice.75
  197.4 4.8 %fusion.38 = f32[16,128,128]{2,1,0:T(8,128)S(1)} fusion(f32[16,128,128]{2,1,0:T(8,128)S(1)} %get-tuple-element.281, s32[]{:T(128)S(6)} %select_n.63, bf16[512,16384]{1,0:T(8,128)(2,1)} %get-tuple-element.306, s32[]{:T(128)S(6)} %select_n.67, bf16[256,16384]{1,0:T(8,128)(2,1)} %get-tuple-element.303, s32[]{:T(128)S(6)} %select_n.68, ...), kind=kOutput, calls=%fused_computation.7.clone.1 | convolution fusion | flops 536920064 | bytes 8455180 | tf_op jit(solution)/shard_map/while/body/dot_general | solution.py:48
  202.8 0.6 fusion.37
  205.7 0.1 dynamic_slice.74
  207.7 0.1 dynamic_slice.75
  207.8 4.8 %fusion.38 = f32[16,128,128]{2,1,0:T(8,128)S(1)} fusion(f32[16,128,128]{2,1,0:T(8,128)S(1)} %get-tuple-element.281, s32[]{:T(128)S(6)} %select_n.63, bf16[512,16384]{1,0:T(8,128)(2,1)} %get-tuple-element.306, s32[]{:T(128)S(6)} %select_n.67, bf16[256,16384]{1,0:T(8,128)(2,1)} %get-tuple-element.303, s32[]{:T(128)S(6)} %select_n.68, ...), kind=kOutput, calls=%fused_computation.7.clone.1 | convolution fusion | flops 536920064 | bytes 8455180 | tf_op jit(solution)/shard_map/while/body/dot_general | solution.py:48
  213.3 0.6 fusion.37
  216.1 0.1 dynamic_slice.74
  218.1 0.1 dynamic_slice.75
  218.2 4.8 %fusion.38 = f32[16,128,128]{2,1,0:T(8,128)S(1)} fusion(f32[16,128,128]{2,1,0:T(8,128)S(1)} %get-tuple-element.281, s32[]{:T(128)S(6)} %select_n.63, bf16[512,16384]{1,0:T(8,128)(2,1)} %get-tuple-element.306, s32[]{:T(128)S(6)} %select_n.67, bf16[256,16384]{1,0:T(8,128)(2,1)} %get-tuple-element.303, s32[]{:T(128)S(6)} %select_n.68, ...), kind=kOutput, calls=%fused_computation.7.clone.1 | convolution fusion | flops 536920064 | bytes 8455180 | tf_op jit(solution)/shard_map/while/body/dot_general | solution.py:48
  223.7 0.6 fusion.37
  226.5 0.1 dynamic_slice.74
  228.5 0.1 dynamic_slice.75
  228.6 4.8 %fusion.38 = f32[16,128,128]{2,1,0:T(8,128)S(1)} fusion(f32[16,128,128]{2,1,0:T(8,128)S(1)} %get-tuple-element.281, s32[]{:T(128)S(6)} %select_n.63, bf16[512,16384]{1,0:T(8,128)(2,1)} %get-tuple-element.306, s32[]{:T(128)S(6)} %select_n.67, bf16[256,16384]{1,0:T(8,128)(2,1)} %get-tuple-element.303, s32[]{:T(128)S(6)} %select_n.68, ...), kind=kOutput, calls=%fused_computation.7.clone.1 | convolution fusion | flops 536920064 | bytes 8455180 | tf_op jit(solution)/shard_map/while/body/dot_general | solution.py:48
  234.1 0.6 fusion.37
  236.9 0.1 dynamic_slice.74
  238.9 0.1 dynamic_slice.75
  239.0 4.8 %fusion.38 = f32[16,128,128]{2,1,0:T(8,128)S(1)} fusion(f32[16,128,128]{2,1,0:T(8,128)S(1)} %get-tuple-element.281, s32[]{:T(128)S(6)} %select_n.63, bf16[512,16384]{1,0:T(8,128)(2,1)} %get-tuple-element.306, s32[]{:T(128)S(6)} %select_n.67, bf16[256,16384]{1,0:T(8,128)(2,1)} %get-tuple-element.303, s32[]{:T(128)S(6)} %select_n.68, ...), kind=kOutput, calls=%fused_computation.7.clone.1 | convolution fusion | flops 536920064 | bytes 8455180 | tf_op jit(solution)/shard_map/while/body/dot_general | solution.py:48
  244.5 0.6 fusion.37
  247.3 0.1 dynamic_slice.74
  249.4 4.8 %fusion.38 = f32[16,128,128]{2,1,0:T(8,128)S(1)} fusion(f32[16,128,128]{2,1,0:T(8,128)S(1)} %get-tuple-element.281, s32[]{:T(128)S(6)} %select_n.63, bf16[512,16384]{1,0:T(8,128)(2,1)} %get-tuple-element.306, s32[]{:T(128)S(6)} %select_n.67, bf16[256,16384]{1,0:T(8,128)(2,1)} %get-tuple-element.303, s32[]{:T(128)S(6)} %select_n.68, ...), kind=kOutput, calls=%fused_computation.7.clone.1 | convolution fusion | flops 536920064 | bytes 8455180 | tf_op jit(solution)/shard_map/while/body/dot_general | solution.py:48
  254.9 0.6 fusion.37
  259.8 4.8 %fusion.38 = f32[16,128,128]{2,1,0:T(8,128)S(1)} fusion(f32[16,128,128]{2,1,0:T(8,128)S(1)} %get-tuple-element.281, s32[]{:T(128)S(6)} %select_n.63, bf16[512,16384]{1,0:T(8,128)(2,1)} %get-tuple-element.306, s32[]{:T(128)S(6)} %select_n.67, bf16[256,16384]{1,0:T(8,128)(2,1)} %get-tuple-element.303, s32[]{:T(128)S(6)} %select_n.68, ...), kind=kOutput, calls=%fused_computation.7.clone.1 | convolution fusion | flops 536920064 | bytes 8455180 | tf_op jit(solution)/shard_map/while/body/dot_general | solution.py:48
  265.3 0.6 fusion.37
  270.2 4.8 %fusion.38 = f32[16,128,128]{2,1,0:T(8,128)S(1)} fusion(f32[16,128,128]{2,1,0:T(8,128)S(1)} %get-tuple-element.281, s32[]{:T(128)S(6)} %select_n.63, bf16[512,16384]{1,0:T(8,128)(2,1)} %get-tuple-element.306, s32[]{:T(128)S(6)} %select_n.67, bf16[256,16384]{1,0:T(8,128)(2,1)} %get-tuple-element.303, s32[]{:T(128)S(6)} %select_n.68, ...), kind=kOutput, calls=%fused_computation.7.clone.1 | convolution fusion | flops 536920064 | bytes 8455180 | tf_op jit(solution)/shard_map/while/body/dot_general | solution.py:48
  275.7 0.6 fusion.37
  280.6 4.8 %fusion.38 = f32[16,128,128]{2,1,0:T(8,128)S(1)} fusion(f32[16,128,128]{2,1,0:T(8,128)S(1)} %get-tuple-element.281, s32[]{:T(128)S(6)} %select_n.63, bf16[512,16384]{1,0:T(8,128)(2,1)} %get-tuple-element.306, s32[]{:T(128)S(6)} %select_n.67, bf16[256,16384]{1,0:T(8,128)(2,1)} %get-tuple-element.303, s32[]{:T(128)S(6)} %select_n.68, ...), kind=kOutput, calls=%fused_computation.7.clone.1 | convolution fusion | flops 536920064 | bytes 8455180 | tf_op jit(solution)/shard_map/while/body/dot_general | solution.py:48
  286.1 0.6 fusion.37
  291.0 4.8 %fusion.38 = f32[16,128,128]{2,1,0:T(8,128)S(1)} fusion(f32[16,128,128]{2,1,0:T(8,128)S(1)} %get-tuple-element.281, s32[]{:T(128)S(6)} %select_n.63, bf16[512,16384]{1,0:T(8,128)(2,1)} %get-tuple-element.306, s32[]{:T(128)S(6)} %select_n.67, bf16[256,16384]{1,0:T(8,128)(2,1)} %get-tuple-element.303, s32[]{:T(128)S(6)} %select_n.68, ...), kind=kOutput, calls=%fused_computation.7.clone.1 | convolution fusion | flops 536920064 | bytes 8455180 | tf_op jit(solution)/shard_map/while/body/dot_general | solution.py:48
  296.5 1.0 copy-done.1
  (20 shorter events, 0.8 us)
Async XLA Ops:
  6.5 117.7 %all-gather.3.cloned.1.call-start = ((), (), s32[]{:S(2)}) async-start(), calls=%async_computation | async-start | bytes 8912896 | tf_op jit(solution)/shard_map/all_gather | solution.py:24
  7.3 13.6 %collective-permute-start = (bf16[256,16384]{1,0:T(8,128)(2,1)}, bf16[256,16384]{1,0:T(8,128)(2,1)}, u32[]{:S(2)}, u32[]{:S(2)}) collective-permute-start(bf16[256,16384]{1,0:T(8,128)(2,1)} %bitcast.18), channel_id=1, source_target_pairs={{0,1},{1,0},{2,3},{3,2},{4,5},{5,4},{6,7},{7,6},{8,9},{9,8},{10,11... | collective-permute-start | bytes 25165832 | tf_op jit(solution)/shard_map/ppermute | solution.py:13
  7.3 20.7 %copy-start = (bf16[1,256,16384]{2,1,0:T(8,128)(2,1)S(1)}, bf16[1,256,16384]{2,1,0:T(8,128)(2,1)}, u32[]{:S(2)}) copy-start(bf16[1,256,16384]{2,1,0:T(8,128)(2,1)} %param.8) | copy-start | bytes 25165828
  28.0 101.4 %copy-start.2 = (s32[1,1,16]{2,1,0:T(1,128)S(1)}, s32[1,1,16]{2,1,0:T(1,128)}, u32[]{:S(2)}) copy-start(s32[1,1,16]{2,1,0:T(1,128)} %param.9) | copy-start | bytes 196
  28.1 101.4 %copy-start.3 = (s32[1,1,16]{2,1,0:T(1,128)S(1)}, s32[1,1,16]{2,1,0:T(1,128)}, u32[]{:S(2)}) copy-start(s32[1,1,16]{2,1,0:T(1,128)} %param.10) | copy-start | bytes 196
  296.5 1.0 copy-start.1
Sparse Core Ops, SparseCore 0:
  10.1 114.0 all-gather.2
where the time goes:
time: 305 us; the launch traced here: 304 us
  waiting for transfers between devices  99.6 us (33%)
  loops' own time  77.8 us (26%)
  matrix products  76.9 us (25%)
  other arithmetic  32.9 us (11%)
  between operations  13.5 us (4%)
  local copies, waits for them, and re-layouts  3.54 us (1%)
    all_gather x1, waiting for transfers between devices, shards(): panel = lax.all_gather(queries[0], 'query', axis=0, tiled=True)  85.4 us
    another operation x1, loops' own time, shards(): lax.fori_loop(0, live_slots, score_slot, jnp.zeros((slot_total, block_row...  77.8 us
    dot_general x16, matrix products, score_slot(): lax.dot_general(query_rows, camera_rows, (((1,), (1,)), ((), ())), prefer...  76.9 us
    ppermute x1, waiting for transfers between devices, passed_along(): lax.ppermute(x, axis, [(i, (i + by) % devices) for i in range(devices)])  13.5 us
    reduce_sum x2, other arithmetic, inverse_rms(): return lax.rsqrt(jnp.mean(wide * wide, axis=-1) + 1e-06)  12.3 us
    concatenate x1, other arithmetic, shards(): camera_stack = jnp.concatenate(tile_list, axis=0)  10.7 us
    mul x16, other arithmetic, score_slot(): camera_global = camera_block[0, 0, slot_index] * block_rows  9.85 us
  transfers between devices with their start and end apart: 2, of which 2 were waited for; matrix products, arithmetic and copies ran while one was open for 6% of the time, Pallas kernels for 0%

commit v1 on v0

v1 whole, which is shorter than its diff:
```python
import math

import jax
import jax.numpy as jnp
from jax import lax
from jax.experimental import pallas as pl
from jax.experimental.pallas import tpu as pltpu
from jax.sharding import PartitionSpec as P

BLOCK = 128
CHUNKS = 8
ORDERS = ("zxy", "zyx", "xyz", "zxy", "zyx", "yxz", "zxy", "zyx")
SUB = 512
MESH = pl.DeviceIdType.MESH


def passed_along(x, axis, by):
    devices = lax.axis_size(axis)
    return lax.ppermute(x, axis, [(i, (i + by) % devices) for i in range(devices)])


def inverse_rms(values):
    wide = values.astype(jnp.float32)
    return lax.rsqrt(jnp.mean(wide * wide, axis=-1) + 1e-06)


def line_shards(queries, cameras, query_block, camera_block, counts):
    feature_count = queries.shape[2]
    panel = lax.all_gather(queries[0], "query", axis=0, tiled=True)
    query_scale = inverse_rms(panel)
    tile_rows = cameras.shape[1]
    core_count = lax.axis_size("blk")
    current = cameras[0]
    tile_list = [current]
    for _ in range(core_count - 1):
        current = passed_along(current, "blk", 1)
        tile_list.append(current)
    camera_stack = jnp.concatenate(tile_list, axis=0)
    camera_scale = inverse_rms(camera_stack)
    my_core = lax.axis_index("blk")
    slot_total = query_block.shape[2]
    inv_root = 1.0 / math.sqrt(feature_count)

    def score_slot(slot_index, results):
        query_start = query_block[0, 0, slot_index] * BLOCK
        camera_global = camera_block[0, 0, slot_index] * BLOCK
        turn = (my_core - camera_global // tile_rows) % core_count
        camera_start = turn * tile_rows + camera_global % tile_rows
        query_rows = lax.dynamic_slice_in_dim(panel, query_start, BLOCK, 0)
        camera_rows = lax.dynamic_slice_in_dim(camera_stack, camera_start, BLOCK, 0)
        products = lax.dot_general(
            query_rows, camera_rows, (((1,), (1,)), ((), ())), preferred_element_type=jnp.float32
        )
        query_norms = lax.dynamic_slice_in_dim(query_scale, query_start, BLOCK, 0)
        camera_norms = lax.dynamic_slice_in_dim(camera_scale, camera_start, BLOCK, 0)
        scored = products * query_norms[:, None] * camera_norms[None, :] * inv_root
        return lax.dynamic_update_index_in_dim(results, scored, slot_index, 0)

    results = lax.fori_loop(
        0, counts[0, 0], score_slot, jnp.zeros((slot_total, BLOCK, BLOCK), jnp.float32)
    )
    return results[None, None]


def box_kernel(
    q_ref, cam_ref, table,
    panel, cams, acc, qacc, cacc,
    local_sem, cam_local_sem, cam_send, cam_recv, recv, send_x, send_y, send_up, send_down, send_fwd,
):
    rows, features = q_ref.shape
    cam_rows = cam_ref.shape[0]
    width = features // CHUNKS
    me = lax.axis_index("query")
    core = lax.axis_index("blk")
    z, y, x = me // 4, (me // 2) % 2, me % 2
    mid = ((z + 1) // 2) % 2 == 1
    near = (z + 1 - 2 * (z % 2), 2 - z // 2, 3 - 3 * (z // 2))
    fwd_z = (3 - z, 3 * (z - 1), 3 * (z - 1))

    def index_of(zz, yy, xx):
        return (zz * 2 + yy) * 2 + xx

    x_peer, y_peer = index_of(z, y, 1 - x), index_of(z, 1 - y, x)
    up, down = me + 4, me - 4

    barrier = pltpu.get_barrier_semaphore()
    pl.semaphore_signal(barrier, inc=1, device_id={"query": x_peer}, device_id_type=MESH)
    pl.semaphore_signal(barrier, inc=1, device_id={"query": y_peer}, device_id_type=MESH)
    pl.semaphore_signal(barrier, inc=1, device_id={"blk": 1 - core}, device_id_type=MESH)

    @pl.when(z < 3)
    def _():
        pl.semaphore_signal(barrier, inc=1, device_id={"query": up}, device_id_type=MESH)

    @pl.when(z > 0)
    def _():
        pl.semaphore_signal(barrier, inc=1, device_id={"query": down}, device_id_type=MESH)

    def own_copy(c):
        return pltpu.make_async_copy(
            q_ref.at[:, pl.ds(c * width, width)],
            panel.at[c, pl.ds(me * rows, rows)],
            local_sem.at[c],
        )

    def cam_local(c):
        return pltpu.make_async_copy(
            cam_ref.at[:, pl.ds(c * width, width)],
            cams.at[c, pl.ds(core * cam_rows, cam_rows)],
            cam_local_sem.at[c],
        )

    def cam_remote(c):
        return pltpu.make_async_remote_copy(
            src_ref=cam_ref.at[:, pl.ds(c * width, width)],
            dst_ref=cams.at[c, pl.ds(core * cam_rows, cam_rows)],
            send_sem=cam_send.at[c],
            recv_sem=cam_recv.at[c],
            device_id={"blk": 1 - core},
            device_id_type=MESH,
        )

    for c in range(CHUNKS):
        own_copy(c).start()

    pl.semaphore_wait(barrier, 4 + ((z + 1) // 2) % 2)

    def block_of(c, owner):
        return panel.at[c, pl.ds(pl.multiple_of(owner * rows, rows), rows)]

    def send(c, owner, sem, target, first=False):
        source = q_ref.at[:, pl.ds(c * width, width)] if first else block_of(c, owner)
        pltpu.make_async_remote_copy(
            src_ref=source,
            dst_ref=block_of(c, owner),
            send_sem=sem.at[c],
            recv_sem=recv.at[c, owner],
            device_id={"query": target},
            device_id_type=MESH,
        ).start()

    def forward(c, owner, dims, first=False):
        if "x" in dims:
            send(c, owner, send_x, x_peer, first)
        if "y" in dims:
            send(c, owner, send_y, y_peer, first)
        if "z" in dims:
            @pl.when(z < 3)
            def _():
                send(c, owner, send_up, up, first)

            @pl.when(z > 0)
            def _():
                send(c, owner, send_down, down, first)

    for c in range(CHUNKS):
        forward(c, me, ORDERS[c], True)
        if c == 1:
            for e in range(CHUNKS):
                cam_remote(e).start()
    for c in range(CHUNKS):
        cam_local(c).start()

    acc[...] = jnp.zeros_like(acc)
    qacc[...] = jnp.zeros_like(qacc)
    cacc[...] = jnp.zeros_like(cacc)

    def squares(ref, c, into, height):
        def step(r, carry):
            at = pl.ds(pl.multiple_of(r * 32, 32), 32)
            total = into[at, :]
            for b in range(width // 128):
                v = ref[c, at, b * 128:(b + 1) * 128].astype(jnp.float32)
                total = total + v * v
            into[at, :] = total
            return carry
        lax.fori_loop(0, height // 32, step, 0)

    def multiply(c):
        def step(b, carry):
            at = pl.ds(pl.multiple_of(b * SUB, SUB), SUB)
            acc[...] += lax.dot_general(
                panel[c, :, at], cams[c, :, at], (((1,), (1,)), ((), ())),
                preferred_element_type=jnp.float32,
            )
            return carry
        lax.fori_loop(0, width // SUB, step, 0)

    def arrived(c, owner):
        pltpu.make_async_copy(block_of(c, owner), block_of(c, owner), recv.at[c, owner]).wait()

    def level(c, h):
        order = ORDERS[c]
        for k in (-1, 0, 1, 2):
            for dx in (0, 1):
                for dy in (0, 1):
                    if k + 1 + dx + dy != h:
                        continue
                    zo = z if k < 0 else near[k]
                    owner = index_of(zo, (y + dy) % 2, (x + dx) % 2)
                    moved = {"z": k >= 0, "x": dx == 1, "y": dy == 1}
                    last = max(i for i in range(3) if moved[order[i]])
                    arrived(c, owner)
                    forward(c, owner, order[last + 1:])
                    if order[last] == "z":
                        @pl.when(mid)
                        def _():
                            send(c, owner, send_fwd, index_of(fwd_z[k], y, x))

    for t in range(CHUNKS + 4):
        for h in (5, 4, 3, 2, 1):
            c = t - (h - 1)
            if 0 <= c < CHUNKS:
                level(c, h)
                if h == 5:
                    own_copy(c).wait()
                    multiply(c)
                    squares(panel, c, qacc, panel.shape[1])
        if t < CHUNKS:
            cam_local(t).wait()
            cam_remote(t).wait_recv()
            squares(cams, t, cacc, cams.shape[1])

    inv_root = 1.0 / math.sqrt(features)
    q_scale = lax.rsqrt(jnp.sum(qacc[...], axis=1, keepdims=True) / features + 1e-06)
    c_sum = jnp.sum(jnp.transpose(cacc[...]), axis=0, keepdims=True)
    c_scale = lax.rsqrt(c_sum / features + 1e-06)
    table[...] = acc[...] * q_scale * c_scale * inv_root

    def drain(c, count, sem):
        part = panel.at[c, pl.ds(0, count * rows)]
        pltpu.make_async_copy(part, part, sem.at[c]).wait()

    for c in range(CHUNKS):
        order = ORDERS[c]
        size = {"x": 2, "y": 2, "z": 4}
        through, total = {}, 1
        for d in order:
            through[d] = total
            total *= size[d]
        drain(c, through["x"], send_x)
        drain(c, through["y"], send_y)
        cam_remote(c).wait_send()

        @pl.when(z < 3)
        def _():
            drain(c, through["z"], send_up)

        @pl.when(z > 0)
        def _():
            drain(c, through["z"], send_down)

        @pl.when(mid)
        def _():
            drain(c, 3 * through["z"], send_fwd)


def pick_kernel(query_block, camera_block, counts, table, out_ref):
    def emit(slot, carry):
        query_at = pl.ds(pl.multiple_of(query_block[slot] * BLOCK, BLOCK), BLOCK)
        camera_at = pl.ds(pl.multiple_of(camera_block[slot] * BLOCK, BLOCK), BLOCK)
        tile = table[query_at, camera_at]
        out_ref[slot] = jnp.where(slot < counts[0], tile, jnp.zeros_like(tile))
        return carry

    lax.fori_loop(0, out_ref.shape[0], emit, 0)


def box_shards(queries, cameras, query_block, camera_block, counts):
    rows, features = queries.shape[1:]
    devices = lax.axis_size("query")
    cam_rows = cameras.shape[1]
    slots = query_block.shape[2]
    width = features // CHUNKS
    smem = pl.BlockSpec(memory_space=pltpu.SMEM)
    hbm = pl.BlockSpec(memory_space=pl.ANY)
    dma = pltpu.SemaphoreType.DMA
    table = pl.pallas_call(
        box_kernel,
        out_shape=jax.ShapeDtypeStruct((devices * rows, 2 * cam_rows), jnp.float32),
        in_specs=[hbm, hbm],
        out_specs=pl.BlockSpec(memory_space=pltpu.VMEM),
        scratch_shapes=[
            pltpu.VMEM((CHUNKS, devices * rows, width), jnp.bfloat16),
            pltpu.VMEM((CHUNKS, 2 * cam_rows, width), jnp.bfloat16),
            pltpu.VMEM((devices * rows, 2 * cam_rows), jnp.float32),
            pltpu.VMEM((devices * rows, 128), jnp.float32),
            pltpu.VMEM((2 * cam_rows, 128), jnp.float32),
            dma((CHUNKS,)),
            dma((CHUNKS,)),
            dma((CHUNKS,)),
            dma((CHUNKS,)),
            dma((CHUNKS, devices)),
            dma((CHUNKS,)),
            dma((CHUNKS,)),
            dma((CHUNKS,)),
            dma((CHUNKS,)),
            dma((CHUNKS,)),
        ],
        compiler_params=pltpu.CompilerParams(
            collective_id=0, has_side_effects=True, vmem_limit_bytes=44 * 1024 * 1024
        ),
        cost_estimate=pl.CostEstimate(flops=2 * 256 * 512 * 16384, bytes_accessed=32 << 20, transcendentals=0),
    )(queries[0], cameras[0])
    out = pl.pallas_call(
        pick_kernel,
        out_shape=jax.ShapeDtypeStruct((slots, BLOCK, BLOCK), jnp.float32),
        in_specs=[smem, smem, smem, pl.BlockSpec(memory_space=pltpu.VMEM)],
        out_specs=pl.BlockSpec(memory_space=pltpu.VMEM),
    )(query_block[0, 0], camera_block[0, 0], counts[0], table)
    return out[None, None]


def solution(mesh):
    placed = (
        P("blk", ("parts", "query"), None),
        P(("parts", "query"), "blk", None),
        P(("parts", "query"), "blk", None),
        P(("parts", "query"), "blk", None),
        P(("parts", "query"), "blk"),
    )
    box = mesh.shape["parts"] == 1 and mesh.shape["query"] == 16 and mesh.shape["blk"] == 2
    return jax.shard_map(
        box_shards if box else line_shards,
        mesh=mesh,
        in_specs=placed,
        out_specs=P(("parts", "query"), "blk", None, None, None),
        check_vma=False,
    )
```

time: 305 us -> 96.9 us (0.32)
  the two profiles are of different devices: /device:TPU:4 before, /device:TPU:0 now
where the time goes in v1:
time: 96.9 us; the launch traced here: 96.7 us
  Pallas kernels  90.8 us (94%)
  local copies, waits for them, and re-layouts  5.2 us (5%)
    pallas_call x1, Pallas kernels, box_shards(): pl.pallas_call(box_kernel, out_shape=jax.ShapeDtypeStruct((devices * rows...  88.5 us
    unnamed x6, local copies, waits for them, and re-layouts  5.2 us
    pallas_call x1, Pallas kernels, box_shards(): pl.pallas_call(pick_kernel, out_shape=jax.ShapeDtypeStruct((slots, BLOCK,...  2.28 us

profile of v1, /device:TPU:0, one launch (start us, length us, event | category | flops | bytes accessed | tf_op | source)
XLA Modules:
  0.0 96.7 jit_solution(14541986752383664623)
XLA Ops:
  0.7 0.0 copy-start.1
  0.7 3.4 %copy-done.1 = bf16[1,256,16384]{2,1,0:T(8,128)(2,1)S(1)} copy-done((bf16[1,256,16384]{2,1,0:T(8,128)(2,1)S(1)}, bf16[1,256,16384]{2,1,0:T(8,128)(2,1)}, u32[]{:S(2)}) %copy-start.1) | copy-done | bytes 8388632
  4.0 0.0 copy-start.2
  4.0 1.0 %copy-done.2 = bf16[1,16,16384]{2,1,0:T(8,128)(2,1)S(1)} copy-done((bf16[1,16,16384]{2,1,0:T(8,128)(2,1)S(1)}, bf16[1,16,16384]{2,1,0:T(8,128)(2,1)}, u32[]{:S(2)}) %copy-start.2) | copy-done | bytes 524312
  5.1 88.5 %shard_map.55.table = f32[256,512]{1,0:T(8,128)S(1)} custom-call(bf16[16,16384]{1,0:T(8,128)(2,1)S(1)} %bitcast.8, bf16[256,16384]{1,0:T(8,128)(2,1)S(1)} %bitcast.7), custom_call_target="tpu_custom_call" | custom-call | flops 4294967296 | bytes 33554432 | tf_op jit(solution)/shard_map/pallas_call | solution.py:278
  93.6 0.0 copy-start
  93.6 0.8 copy-done
  94.4 2.3 %shard_map.56 = f32[16,128,128]{2,1,0:T(8,128)} custom-call(s32[16]{0:T(128)} %bitcast.9, s32[16]{0:T(128)} %bitcast.10, s32[1]{0:T(128)} %bitcast.6.counts, f32[256,512]{1,0:T(8,128)} %copy-done), custom_call_target="tpu_custom_call" | custom-call | tf_op jit(solution)/shard_map/pallas_call | solution.py:305
Async XLA Ops:
  0.7 3.4 %copy-start.1 = (bf16[1,256,16384]{2,1,0:T(8,128)(2,1)S(1)}, bf16[1,256,16384]{2,1,0:T(8,128)(2,1)}, u32[]{:S(2)}) copy-start(bf16[1,256,16384]{2,1,0:T(8,128)(2,1)} %param.6) | copy-start | bytes 25165828
  4.0 1.0 %copy-start.2 = (bf16[1,16,16384]{2,1,0:T(8,128)(2,1)S(1)}, bf16[1,16,16384]{2,1,0:T(8,128)(2,1)}, u32[]{:S(2)}) copy-start(bf16[1,16,16384]{2,1,0:T(8,128)(2,1)} %param.5) | copy-start | bytes 1572868
  93.6 0.8 copy-start

commit v2 on v1

--- a/solution.py
+++ b/solution.py
@@ -8,8 +8,8 @@
 from jax.sharding import PartitionSpec as P
 
 BLOCK = 128
-CHUNKS = 8
-ORDERS = ("zxy", "zyx", "xyz", "zxy", "zyx", "yxz", "zxy", "zyx")
+CHUNKS = 16
+ORDERS = ("zxy", "zyx", "xyz", "zxy", "zyx", "yxz", "zxy", "zyx") * 2
 SUB = 512
 MESH = pl.DeviceIdType.MESH
 
@@ -273,7 +273,7 @@
     slots = query_block.shape[2]
     width = features // CHUNKS
     smem = pl.BlockSpec(memory_space=pltpu.SMEM)
-    hbm = pl.BlockSpec(memory_space=pl.ANY)
+    hbm = pl.BlockSpec(memory_space=pltpu.HBM)
     dma = pltpu.SemaphoreType.DMA
     table = pl.pallas_call(
         box_kernel,

time: 96.9 us -> 117 us (1.21)
  Pallas kernels: 90.8 us -> 111 us
    pallas_call x1, Pallas kernels: 88.5 us -> 109 us  [box_shards(): pl.pallas_call(box_kernel, out_shape=jax.ShapeDtypeStruct((devices * rows...]
where the time goes in v2:
time: 117 us
  Pallas kernels  111 us (95%)
  local copies, waits for them, and re-layouts  5.2 us (4%)
    pallas_call x1, Pallas kernels, box_shards(): pl.pallas_call(box_kernel, out_shape=jax.ShapeDtypeStruct((devices * rows...  109 us
    unnamed x6, local copies, waits for them, and re-layouts  5.2 us

profile of v2, /device:TPU:0, one launch (start us, length us, event | category | flops | bytes accessed | tf_op | source)
XLA Modules:
  0.0 116.9 jit_solution(8537528035610470940)
XLA Ops:
  0.7 0.0 copy-start.1
  0.7 3.4 %copy-done.1 = bf16[1,256,16384]{2,1,0:T(8,128)(2,1)S(1)} copy-done((bf16[1,256,16384]{2,1,0:T(8,128)(2,1)S(1)}, bf16[1,256,16384]{2,1,0:T(8,128)(2,1)}, u32[]{:S(2)}) %copy-start.1) | copy-done | bytes 8388632
  4.0 0.0 copy-start.2
  4.0 1.0 copy-done.2
  5.1 108.7 %shard_map.55.table = f32[256,512]{1,0:T(8,128)S(1)} custom-call(bf16[16,16384]{1,0:T(8,128)(2,1)S(1)} %bitcast.8, bf16[256,16384]{1,0:T(8,128)(2,1)S(1)} %bitcast.7), custom_call_target="tpu_custom_call" | custom-call | flops 4294967296 | bytes 33554432 | tf_op jit(solution)/shard_map/pallas_call | solution.py:278
  113.8 0.0 copy-start
  113.8 0.8 copy-done
  114.6 2.3 %shard_map.56 = f32[16,128,128]{2,1,0:T(8,128)} custom-call(s32[16]{0:T(128)} %bitcast.9, s32[16]{0:T(128)} %bitcast.10, s32[1]{0:T(128)} %bitcast.6.counts, f32[256,512]{1,0:T(8,128)} %copy-done), custom_call_target="tpu_custom_call" | custom-call | tf_op jit(solution)/shard_map/pallas_call | solution.py:305
Async XLA Ops:
  0.7 3.4 %copy-start.1 = (bf16[1,256,16384]{2,1,0:T(8,128)(2,1)S(1)}, bf16[1,256,16384]{2,1,0:T(8,128)(2,1)}, u32[]{:S(2)}) copy-start(bf16[1,256,16384]{2,1,0:T(8,128)(2,1)} %param.6) | copy-start | bytes 25165828
  4.0 1.0 copy-start.2
  113.8 0.8 copy-start

commit v3 on v2

--- a/solution.py
+++ b/solution.py
@@ -11,6 +11,7 @@
 CHUNKS = 16
 ORDERS = ("zxy", "zyx", "xyz", "zxy", "zyx", "yxz", "zxy", "zyx") * 2
 SUB = 512
+WAITS = {"z": (0, 1, 2, 4, 6), "x": (0, 2, 4, 5, 6), "y": (0, 2, 4, 5, 6)}
 MESH = pl.DeviceIdType.MESH
 
 
@@ -96,10 +97,45 @@
     def _():
         pl.semaphore_signal(barrier, inc=1, device_id={"query": down}, device_id_type=MESH)
 
+    def place(c, zz, yy, xx):
+        order = ORDERS[c]
+        first, second = (yy, xx) if "xy" in order else (xx, yy)
+        if order[0] == "z":
+            return (first * 2 + second) * 4 + zz
+        return (zz * 2 + first) * 2 + second
+
+    def block_of(c, slot, count=1):
+        return panel.at[c, pl.ds(pl.multiple_of(slot * rows, rows), count * rows)]
+
+    def send(c, slot, count, sem, message, target, first=False):
+        pltpu.make_async_remote_copy(
+            src_ref=q_ref.at[:, pl.ds(c * width, width)] if first else block_of(c, slot, count),
+            dst_ref=block_of(c, slot, count),
+            send_sem=sem.at[c],
+            recv_sem=recv.at[c, message],
+            device_id={"query": target},
+            device_id_type=MESH,
+        ).start()
+
+    def send_line(c, slot, count, first=False):
+        @pl.when(z < 3)
+        def _():
+            send(c, slot, count, send_up, z, up, first)
+
+        @pl.when(z > 0)
+        def _():
+            send(c, slot, count, send_down, z, down, first)
+
+    across = {"x": (send_x, x_peer), "y": (send_y, y_peer)}
+
+    def send_across(c, d, slot, count, message, first=False):
+        sem, peer = across[d]
+        send(c, slot, count, sem, message, peer, first)
+
     def own_copy(c):
         return pltpu.make_async_copy(
             q_ref.at[:, pl.ds(c * width, width)],
-            panel.at[c, pl.ds(me * rows, rows)],
+            block_of(c, place(c, z, y, x)),
             local_sem.at[c],
         )
 
@@ -125,36 +161,11 @@
 
     pl.semaphore_wait(barrier, 4 + ((z + 1) // 2) % 2)
 
-    def block_of(c, owner):
-        return panel.at[c, pl.ds(pl.multiple_of(owner * rows, rows), rows)]
-
-    def send(c, owner, sem, target, first=False):
-        source = q_ref.at[:, pl.ds(c * width, width)] if first else block_of(c, owner)
-        pltpu.make_async_remote_copy(
-            src_ref=source,
-            dst_ref=block_of(c, owner),
-            send_sem=sem.at[c],
-            recv_sem=recv.at[c, owner],
-            device_id={"query": target},
-            device_id_type=MESH,
-        ).start()
-
-    def forward(c, owner, dims, first=False):
-        if "x" in dims:
-            send(c, owner, send_x, x_peer, first)
-        if "y" in dims:
-            send(c, owner, send_y, y_peer, first)
-        if "z" in dims:
-            @pl.when(z < 3)
-            def _():
-                send(c, owner, send_up, up, first)
-
-            @pl.when(z > 0)
-            def _():
-                send(c, owner, send_down, down, first)
-
     for c in range(CHUNKS):
-        forward(c, me, ORDERS[c], True)
+        if ORDERS[c][0] == "z":
+            send_line(c, place(c, z, y, x), 1, True)
+        else:
+            send_across(c, ORDERS[c][0], place(c, z, y, x), 1, 4, True)
         if c == 1:
             for e in range(CHUNKS):
                 cam_remote(e).start()
@@ -165,61 +176,82 @@
     qacc[...] = jnp.zeros_like(qacc)
     cacc[...] = jnp.zeros_like(cacc)
 
-    def squares(ref, c, into, height):
+    def squares(ref, c, into, height, row_of):
         def step(r, carry):
-            at = pl.ds(pl.multiple_of(r * 32, 32), 32)
+            at = pl.ds(pl.multiple_of(r * rows, rows), rows)
+            src = pl.ds(pl.multiple_of(row_of(r) * rows, rows), rows)
             total = into[at, :]
             for b in range(width // 128):
-                v = ref[c, at, b * 128:(b + 1) * 128].astype(jnp.float32)
+                v = ref[c, src, b * 128:(b + 1) * 128].astype(jnp.float32)
                 total = total + v * v
             into[at, :] = total
             return carry
-        lax.fori_loop(0, height // 32, step, 0)
+        lax.fori_loop(0, height // rows, step, 0, unroll=4)
 
     def multiply(c):
+        slots = [place(c, i // 4, (i // 2) % 2, i % 2) for i in range(16)]
+
         def step(b, carry):
             at = pl.ds(pl.multiple_of(b * SUB, SUB), SUB)
+            left = jnp.concatenate([panel[c, s * rows:(s + 1) * rows, at] for s in slots], axis=0)
             acc[...] += lax.dot_general(
-                panel[c, :, at], cams[c, :, at], (((1,), (1,)), ((), ())),
+                left, cams[c, :, at], (((1,), (1,)), ((), ())),
                 preferred_element_type=jnp.float32,
             )
             return carry
         lax.fori_loop(0, width // SUB, step, 0)
 
-    def arrived(c, owner):
-        pltpu.make_async_copy(block_of(c, owner), block_of(c, owner), recv.at[c, owner]).wait()
-
-    def level(c, h):
+    def arrived(c, slot, count, message):
+        part = block_of(c, slot, count)
+        pltpu.make_async_copy(part, part, recv.at[c, message]).wait()
+
+    def from_line(c, k, slot, count):
+        arrived(c, slot, count, near[k])
+
+        @pl.when(mid)
+        def _():
+            send(c, slot, count, send_fwd, near[k], index_of(fwd_z[k], y, x))
+
+    def event(c, h):
         order = ORDERS[c]
-        for k in (-1, 0, 1, 2):
-            for dx in (0, 1):
-                for dy in (0, 1):
-                    if k + 1 + dx + dy != h:
-                        continue
-                    zo = z if k < 0 else near[k]
-                    owner = index_of(zo, (y + dy) % 2, (x + dx) % 2)
-                    moved = {"z": k >= 0, "x": dx == 1, "y": dy == 1}
-                    last = max(i for i in range(3) if moved[order[i]])
-                    arrived(c, owner)
-                    forward(c, owner, order[last + 1:])
-                    if order[last] == "z":
-                        @pl.when(mid)
-                        def _():
-                            send(c, owner, send_fwd, index_of(fwd_z[k], y, x))
-
-    for t in range(CHUNKS + 4):
-        for h in (5, 4, 3, 2, 1):
-            c = t - (h - 1)
-            if 0 <= c < CHUNKS:
-                level(c, h)
-                if h == 5:
+        line_first = order[0] == "z"
+        a, b = order.replace("z", "")
+        at = {"x": x, "y": y}
+        other = {"x": 1 - x, "y": 1 - y}
+        if line_first:
+            if h < 3:
+                from_line(c, h, place(c, near[h], y, x), 1)
+                if h == 2:
                     own_copy(c).wait()
-                    multiply(c)
-                    squares(panel, c, qacc, panel.shape[1])
+                    send_across(c, a, (at[b] * 2 + at[a]) * 4, 4, 4)
+            elif h == 3:
+                arrived(c, (at[b] * 2 + other[a]) * 4, 4, 4)
+                send_across(c, b, at[b] * 8, 8, 5)
+            else:
+                arrived(c, other[b] * 8, 8, 5)
+        elif h == 0:
+            own_copy(c).wait()
+            arrived(c, (z * 2 + at[b]) * 2 + other[a], 1, 4)
+            send_across(c, b, (z * 2 + at[b]) * 2, 2, 5)
+        elif h == 1:
+            arrived(c, (z * 2 + other[b]) * 2, 2, 5)
+            send_line(c, z * 4, 4)
+        else:
+            from_line(c, h - 2, near[h - 2] * 4, 4)
+
+    for t in range(CHUNKS + WAITS["z"][-1]):
+        for h in (4, 3, 2, 1, 0):
+            for c in range(CHUNKS):
+                if c + WAITS[ORDERS[c][0]][h] == t:
+                    event(c, h)
+                    if h == 4:
+                        multiply(c)
+                        squares(panel, c, qacc, panel.shape[1],
+                                lambda r: place(c, r // 4, (r // 2) % 2, r % 2))
         if t < CHUNKS:
             cam_local(t).wait()
             cam_remote(t).wait_recv()
-            squares(cams, t, cacc, cams.shape[1])
+            squares(cams, t, cacc, cams.shape[1], lambda r: r)
 
     inv_root = 1.0 / math.sqrt(features)
     q_scale = lax.rsqrt(jnp.sum(qacc[...], axis=1, keepdims=True) / features + 1e-06)
@@ -290,7 +322,7 @@
             dma((CHUNKS,)),
             dma((CHUNKS,)),
             dma((CHUNKS,)),
-            dma((CHUNKS, devices)),
+            dma((CHUNKS, 6)),
             dma((CHUNKS,)),
             dma((CHUNKS,)),
             dma((CHUNKS,)),
@@ -298,7 +330,7 @@
             dma((CHUNKS,)),
         ],
         compiler_params=pltpu.CompilerParams(
-            collective_id=0, has_side_effects=True, vmem_limit_bytes=44 * 1024 * 1024
+            collective_id=0, has_side_effects=True, vmem_limit_bytes=60 * 1024 * 1024
         ),
         cost_estimate=pl.CostEstimate(flops=2 * 256 * 512 * 16384, bytes_accessed=32 << 20, transcendentals=0),
     )(queries[0], cameras[0])

time: 117 us -> 97.7 us (0.84)
  Pallas kernels: 111 us -> 96.9 us
  local copies, waits for them, and re-layouts: 5.2 us -> 0 us
    pallas_call x1, Pallas kernels: 109 us -> 94.6 us  [box_shards(): pl.pallas_call(box_kernel, out_shape=jax.ShapeDtypeStruct((devices * rows...]
    unnamed x6 -> x0, local copies, waits for them, and re-layouts: 5.2 us -> none
where the time goes in v3:
time: 97.7 us; the launch traced here: 97.6 us
  Pallas kernels  96.9 us (99%)
    pallas_call x1, Pallas kernels, box_shards(): pl.pallas_call(box_kernel, out_shape=jax.ShapeDtypeStruct((devices * rows...  94.6 us
    pallas_call x1, Pallas kernels, box_shards(): pl.pallas_call(pick_kernel, out_shape=jax.ShapeDtypeStruct((slots, BLOCK,...  2.29 us

profile of v3, /device:TPU:0, one launch (start us, length us, event | category | flops | bytes accessed | tf_op | source)
XLA Modules:
  0.0 97.6 jit_solution(76345400152753543)
XLA Ops:
  0.7 94.6 %shard_map.55.table = f32[256,512]{1,0:T(8,128)} custom-call(bf16[16,16384]{1,0:T(8,128)(2,1)} %bitcast.10, bf16[256,16384]{1,0:T(8,128)(2,1)} %bitcast.9), custom_call_target="tpu_custom_call" | custom-call | flops 4294967296 | bytes 33554432 | tf_op jit(solution)/shard_map/pallas_call | solution.py:310
  95.3 2.3 %shard_map.56 = f32[16,128,128]{2,1,0:T(8,128)} custom-call(s32[16]{0:T(128)} %bitcast.7, s32[16]{0:T(128)} %bitcast.8, s32[1]{0:T(128)} %bitcast.6.counts, f32[256,512]{1,0:T(8,128)} %shard_map.55.table), custom_call_target="tpu_custom_call" | custom-call | tf_op jit(solution)/shard_map/pallas_call | solution.py:337

commit v4 on v3

--- a/solution.py
+++ b/solution.py
@@ -11,7 +11,7 @@
 CHUNKS = 16
 ORDERS = ("zxy", "zyx", "xyz", "zxy", "zyx", "yxz", "zxy", "zyx") * 2
 SUB = 512
-WAITS = {"z": (0, 1, 2, 4, 6), "x": (0, 2, 4, 5, 6), "y": (0, 2, 4, 5, 6)}
+WAITS = {"z": (1, 3, 6, 10, 14), "x": (1, 5, 9, 12, 14), "y": (1, 5, 9, 12, 14)}
 MESH = pl.DeviceIdType.MESH
 
 

time: 97.7 us -> 83.6 us (0.86)
  Pallas kernels: 96.9 us -> 82.8 us
    pallas_call x1, Pallas kernels: 94.6 us -> 80.5 us  [box_shards(): pl.pallas_call(box_kernel, out_shape=jax.ShapeDtypeStruct((devices * rows...]
where the time goes in v4:
time: 83.6 us; the launch traced here: 83.4 us
  Pallas kernels  82.8 us (99%)
    pallas_call x1, Pallas kernels, box_shards(): pl.pallas_call(box_kernel, out_shape=jax.ShapeDtypeStruct((devices * rows...  80.5 us
    pallas_call x1, Pallas kernels, box_shards(): pl.pallas_call(pick_kernel, out_shape=jax.ShapeDtypeStruct((slots, BLOCK,...  2.29 us

profile of v4, /device:TPU:0, one launch (start us, length us, event | category | flops | bytes accessed | tf_op | source)
XLA Modules:
  0.0 83.4 jit_solution(4163667300705109647)
XLA Ops:
  0.7 80.5 %shard_map.55.table = f32[256,512]{1,0:T(8,128)} custom-call(bf16[16,16384]{1,0:T(8,128)(2,1)} %bitcast.10, bf16[256,16384]{1,0:T(8,128)(2,1)} %bitcast.9), custom_call_target="tpu_custom_call" | custom-call | flops 4294967296 | bytes 33554432 | tf_op jit(solution)/shard_map/pallas_call | solution.py:310
  81.1 2.3 %shard_map.56 = f32[16,128,128]{2,1,0:T(8,128)} custom-call(s32[16]{0:T(128)} %bitcast.7, s32[16]{0:T(128)} %bitcast.8, s32[1]{0:T(128)} %bitcast.6.counts, f32[256,512]{1,0:T(8,128)} %shard_map.55.table), custom_call_target="tpu_custom_call" | custom-call | tf_op jit(solution)/shard_map/pallas_call | solution.py:337

commit v5 on v4

--- a/solution.py
+++ b/solution.py
@@ -10,7 +10,7 @@
 BLOCK = 128
 CHUNKS = 16
 ORDERS = ("zxy", "zyx", "xyz", "zxy", "zyx", "yxz", "zxy", "zyx") * 2
-SUB = 512
+SUB = 1024
 WAITS = {"z": (1, 3, 6, 10, 14), "x": (1, 5, 9, 12, 14), "y": (1, 5, 9, 12, 14)}
 MESH = pl.DeviceIdType.MESH
 

time: 83.6 us -> 83.4 us (level)
  no operation moved by 1% of the time
where the time goes in v5:
time: 83.4 us; the launch traced here: 83.2 us
  Pallas kernels  82.6 us (99%)
    pallas_call x1, Pallas kernels, box_shards(): pl.pallas_call(box_kernel, out_shape=jax.ShapeDtypeStruct((devices * rows...  80.3 us
    pallas_call x1, Pallas kernels, box_shards(): pl.pallas_call(pick_kernel, out_shape=jax.ShapeDtypeStruct((slots, BLOCK,...  2.29 us

profile of v5, /device:TPU:0, one launch (start us, length us, event | category | flops | bytes accessed | tf_op | source)
XLA Modules:
  0.0 83.2 jit_solution(12151325565098181853)
XLA Ops:
  0.7 80.3 %shard_map.55.table = f32[256,512]{1,0:T(8,128)} custom-call(bf16[16,16384]{1,0:T(8,128)(2,1)} %bitcast.10, bf16[256,16384]{1,0:T(8,128)(2,1)} %bitcast.9), custom_call_target="tpu_custom_call" | custom-call | flops 4294967296 | bytes 33554432 | tf_op jit(solution)/shard_map/pallas_call | solution.py:310
  80.9 2.3 %shard_map.56 = f32[16,128,128]{2,1,0:T(8,128)} custom-call(s32[16]{0:T(128)} %bitcast.7, s32[16]{0:T(128)} %bitcast.8, s32[1]{0:T(128)} %bitcast.6.counts, f32[256,512]{1,0:T(8,128)} %shard_map.55.table), custom_call_target="tpu_custom_call" | custom-call | tf_op jit(solution)/shard_map/pallas_call | solution.py:337
